TPU v7x, 32 devices: a whole 2x2x4 slice. The times are simulated.
32 devices in a mesh: pulse: 4 (over z), tile: 8 (over y, x, core).
Axes of the slice: x: 2, y: 2, z: 4, core: 2. Of those that a mesh axis runs over, the one named last changes fastest.
Arguments:
- raw: bfloat16 [2, 128, 2048], P(None, ('pulse', 'tile')), may hold values from -6 to 6
- filt: bfloat16 [2, 1024, 2048], replicated, may hold values from -0.125 to 0.125
- range_off: int32 [128], P(('pulse', 'tile')), may hold values from 0 to 1024
- fine: int32 [128], P(('pulse', 'tile')), may hold values from 0 to 3
- dop: int32 [128], P(('pulse', 'tile')), may hold values from 0 to 511
- pulse_order: int32 [32, 4], P(('pulse', 'tile')), may hold values from 0 to 3, each once within a row
- band_idx: int32 [8, 128], P(None, ('pulse', 'tile')), may hold values from 0 to 1023
Outputs:
- image: bfloat16 [2, 512, 32768], P(None, 'pulse', 'tile')
Inputs may be any that keep to these rules, and one draw needn't show every extreme that they name: `pulse_order`: each row is a permutation of 0 .. 3.
All inputs are finite; a program needn't handle non-finite values.
Results may differ from a plain program's by a relative error of at most 0.0065.
Values may be sent and summed in bfloat16 or wider, within the bound.
A program may use at most 192 MiB of HBM per device.

v0:
```python
import jax
import jax.numpy as jnp
from jax import lax
from jax.sharding import PartitionSpec as P

BAND = 1024
STEPS = 4
PS = 1
R_DEV = 128


def compress(windows, filt):
    wr = windows[:, 0]
    wi = windows[:, 1]
    prof_re = jnp.dot(wr, filt[0], preferred_element_type=jnp.float32) - jnp.dot(
        wi, filt[1], preferred_element_type=jnp.float32
    )
    prof_im = jnp.dot(wr, filt[1], preferred_element_type=jnp.float32) + jnp.dot(
        wi, filt[0], preferred_element_type=jnp.float32
    )
    return jnp.stack([prof_re, prof_im], 1).astype(jnp.bfloat16)


def cut_band(profile, start):
    segment = lax.dynamic_slice_in_dim(profile, start, BAND + 1, 1)
    return (segment[:, :BAND], segment[:, BAND])


def interpolate(pieces, edges, shifts):
    first = pieces.astype(jnp.float32)
    second = jnp.concatenate([first[..., 1:], edges.astype(jnp.float32)[..., None]], -1)
    first = jnp.repeat(first, 4, axis=-1)
    second = jnp.repeat(second, 4, axis=-1)
    phase_q = (jnp.arange(4 * BAND, dtype=jnp.int32) % 4).astype(jnp.float32)
    weight = (4.0 * phase_q[None, :] + shifts.astype(jnp.float32)[:, None]) / 16.0
    weight = weight[:, None, :]
    return first * (1.0 - weight) + second * weight


def gradient_terms(samples, summed):
    sr = samples[:, 0]
    si = samples[:, 1]
    g_re = jnp.sum(sr * summed[None, 0] + si * summed[None, 1], axis=-1)
    g_im = jnp.sum(si * summed[None, 0] - sr * summed[None, 1], axis=-1)
    return (g_re, g_im)


def shards(raw, filt, range_off, fine, dop, pulse_order, band_idx):
    n_pulse = lax.axis_size("pulse")
    n_tile = lax.axis_size("tile")
    devices = n_pulse * n_tile
    pulse_index = lax.axis_index("pulse")
    p_dev = raw.shape[1]
    win = filt.shape[1]
    pulses = p_dev * devices
    total_rows = R_DEV * n_pulse
    cols = 4 * BAND
    all_order, all_dop, all_fine = (
        lax.all_gather(pulse_order, ("pulse", "tile"), axis=0, tiled=True),
        lax.all_gather(dop, ("pulse", "tile"), axis=0, tiled=True),
        lax.all_gather(fine, ("pulse", "tile"), axis=0, tiled=True),
    )
    owners = jnp.arange(devices, dtype=jnp.int32)[:, None] * p_dev
    rows_here = pulse_index * R_DEV + jnp.arange(R_DEV, dtype=jnp.int32)
    accumulated = jnp.zeros((2, R_DEV, cols), jnp.float32)
    for step in range(STEPS):
        local_sel = pulse_order[0, step * PS : (step + 1) * PS]
        picked = jnp.take(raw, local_sel, axis=1)
        offsets = jnp.take(range_off, local_sel)
        windows = jax.vmap(
            lambda row, off: lax.dynamic_slice_in_dim(row, off, win, 1), in_axes=(1, 0)
        )(picked, offsets)
        profile = compress(windows, filt)
        chosen = (owners + all_order[:, step * PS : (step + 1) * PS]).reshape(-1)
        starts = jnp.take(band_idx, local_sel, axis=1)
        pieces, edges = jax.vmap(jax.vmap(cut_band, in_axes=(0, 0)), in_axes=(None, 0))(
            profile, starts
        )
        pieces = pieces.reshape(n_tile * PS, 2, BAND)
        edges = edges.reshape(n_tile * PS, 2)
        mine_pieces, mine_edges = (
            lax.all_to_all(pieces, "tile", split_axis=0, concat_axis=0, tiled=True),
            lax.all_to_all(edges, "tile", split_axis=0, concat_axis=0, tiled=True),
        )
        pieces, edges = (
            lax.all_gather(mine_pieces, "pulse", axis=0, tiled=True),
            lax.all_gather(mine_edges, "pulse", axis=0, tiled=True),
        )
        shifts = jnp.take(all_fine, chosen)
        samples = interpolate(pieces, edges, shifts)
        summed = jnp.sum(samples, axis=0)
        g_re, g_im = gradient_terms(samples, summed)
        g_re, g_im = lax.psum((g_re, g_im), "tile")
        scale = jnp.sqrt(g_re * g_re + g_im * g_im + 1.0)
        c_re = (g_re / scale)[:, None]
        c_im = (-g_im / scale)[:, None]
        sr = samples[:, 0]
        si = samples[:, 1]
        right = jnp.concatenate([c_re * sr - c_im * si, c_re * si + c_im * sr], 0).astype(
            jnp.bfloat16
        )
        dops = jnp.take(all_dop, chosen)
        angle = (
            2.0
            * jnp.pi
            * (dops[:, None] * rows_here[None, :] % total_rows).astype(jnp.float32)
            / total_rows
        )
        norm_scale = jnp.sqrt(jnp.float32(pulses))
        e_re = (jnp.cos(angle) / norm_scale).astype(jnp.bfloat16)
        e_im = (jnp.sin(angle) / norm_scale).astype(jnp.bfloat16)
        left = jnp.stack([jnp.concatenate([e_re, -e_im], 0), jnp.concatenate([e_im, e_re], 0)], 0)
        accumulated = accumulated + jnp.einsum(
            "zkr,kc->zrc", left, right, preferred_element_type=jnp.float32
        )
    return accumulated.astype(jnp.bfloat16)


def solution(mesh):
    return jax.shard_map(
        shards,
        mesh=mesh,
        in_specs=(
            P(None, ("pulse", "tile"), None),
            P(),
            P(("pulse", "tile")),
            P(("pulse", "tile")),
            P(("pulse", "tile")),
            P(("pulse", "tile"), None),
            P(None, ("pulse", "tile")),
        ),
        out_specs=P(None, "pulse", "tile"),
        check_vma=False,
    )
```

profile of v0, /device:TPU:0, one launch (start us, length us, event | category | flops | bytes accessed | tf_op | source)
XLA Modules:
  0.0 478.1 jit_solution(11086329522314578801)
XLA Ops:
  13.9 3.0 fusion.19
  16.9 3.3 fusion.3
  21.8 10.7 %while.17 = (s32[]{:T(128)}, bf16[1,2,2048]{2,1,0:T(2,128)(2,1)S(1)}, s32[8,3]{0,1:T(4,128)S(1)}, bf16[8,2,1025]{2,1,0:T(2,128)(2,1)S(1)}, s32[]{:T(128)}) while((s32[]{:T(128)}, bf16[1,2,2048]{2,1,0:T(2,128)(2,1)S(1)}, s32[8,3]{0,1:T(4,128)S(1)}, bf16[8,2,1025]{2,1,0:T(2,128)(2,1)S(1)}, s32[]{:T(128)}) %tuple.191), condition=%wide.while_cond.13, body=%wide.while_body.13.sunk | while | flops 2 | bytes 9321 | solution.py:25
  33.3 5.2 %all-to-all-start.7 = ((bf16[8,1,2]{2,1,0:T(2,128)(2,1)}), bf16[8,1,2]{2,1,0:T(2,128)(2,1)S(1)}, u32[]{:S(2)}, u32[]{:S(2)}) async-start(bf16[8,1,2]{2,1,0:T(2,128)(2,1)} %copy.117), calls=%async_computation.7 | async-start | bytes 8192 | tf_op jit(solution)/shard_map/all_to_all | solution.py:83
  39.1 42.3 %all-gather.4 = s32[32,1,4]{2,1,0:T(1,128)S(1)} all-gather(s32[1,1,4]{2,1,0:T(1,128)S(1)} %bitcast.332), channel_id=1, replica_groups=mesh['pulse'=4,'tile'=8] {'pulse','tile'}, dimensions={0}, use_global_device_ids=true | all-gather | bytes 528 | tf_op jit(solution)/shard_map/all_gather | solution.py:59
  82.0 37.2 %all-reduce.6 = (s32[128]{0:T(128)S(1)}, s32[128]{0:T(128)S(1)}) all-reduce(s32[128]{0:T(128)S(1)} %dynamic-update-slice.19, s32[128]{0:T(128)S(1)} %dynamic-update-slice.18), channel_id=1, replica_groups=mesh['pulse'=4,'tile'=8] {'pulse','tile'}, use_global_device_ids=true, to_apply=%add.5 | all-reduce | flops 256 | bytes 2048
  127.8 2.8 fusion.7
  130.6 2.8 fusion.5
  133.4 2.8 fusion.21
  136.4 10.9 %while.16 = (s32[]{:T(128)}, bf16[1,2,2048]{2,1,0:T(2,128)(2,1)S(1)}, s32[8,3]{0,1:T(4,128)S(1)}, bf16[8,2,1025]{2,1,0:T(2,128)(2,1)S(1)}, s32[]{:T(128)}) while((s32[]{:T(128)}, bf16[1,2,2048]{2,1,0:T(2,128)(2,1)S(1)}, s32[8,3]{0,1:T(4,128)S(1)}, bf16[8,2,1025]{2,1,0:T(2,128)(2,1)S(1)}, s32[]{:T(128)}) %tuple.188), condition=%wide.while_cond.10, body=%wide.while_body.10.sunk | while | flops 2 | bytes 9321 | solution.py:25
  150.8 2.8 fusion.11
  153.6 2.8 fusion.9
  156.4 2.8 fusion.25
  159.4 11.5 %while.15 = (s32[]{:T(128)}, bf16[1,2,2048]{2,1,0:T(2,128)(2,1)S(1)}, s32[8,3]{0,1:T(4,128)S(1)}, bf16[8,2,1025]{2,1,0:T(2,128)(2,1)S(1)}, s32[]{:T(128)}) while((s32[]{:T(128)}, bf16[1,2,2048]{2,1,0:T(2,128)(2,1)S(1)}, s32[8,3]{0,1:T(4,128)S(1)}, bf16[8,2,1025]{2,1,0:T(2,128)(2,1)S(1)}, s32[]{:T(128)}) %tuple.185), condition=%wide.while_cond.7, body=%wide.while_body.7.sunk | while | flops 2 | bytes 9321 | solution.py:25
  174.4 2.8 fusion.15
  177.3 2.8 fusion.13
  180.1 2.8 fusion.29
  183.1 11.3 %while.14 = (s32[]{:T(128)}, bf16[1,2,2048]{2,1,0:T(2,128)(2,1)S(1)}, s32[8,3]{0,1:T(4,128)S(1)}, bf16[8,2,1025]{2,1,0:T(2,128)(2,1)S(1)}, s32[]{:T(128)}) while((s32[]{:T(128)}, bf16[1,2,2048]{2,1,0:T(2,128)(2,1)S(1)}, s32[8,3]{0,1:T(4,128)S(1)}, bf16[8,2,1025]{2,1,0:T(2,128)(2,1)S(1)}, s32[]{:T(128)}) %tuple.182), condition=%wide.while_cond.4, body=%wide.while_body.4.sunk | while | flops 2 | bytes 9321 | solution.py:25
  219.4 15.0 %all-to-all-start.5 = ((bf16[8,1,2]{2,1,0:T(2,128)(2,1)}), bf16[8,1,2]{2,1,0:T(2,128)(2,1)S(1)}, u32[]{:S(2)}, u32[]{:S(2)}) async-start(bf16[8,1,2]{2,1,0:T(2,128)(2,1)} %copy.107), calls=%async_computation.5 | async-start | bytes 8192 | tf_op jit(solution)/shard_map/all_to_all | solution.py:83
  234.4 13.8 %all-gather.3 = bf16[32,1,2]{2,1,0:T(2,128)(2,1)S(1)} all-gather(bf16[8,1,2]{2,1,0:T(2,128)(2,1)S(1)} %all-to-all-done.7), channel_id=5, replica_groups=mesh['pulse'=4,'tile'=8] {'pulse'}, dimensions={0}, use_global_device_ids=true | all-gather | bytes 160 | tf_op jit(solution)/shard_map/all_gather | solution.py:87
  248.3 4.1 all-to-all-start.3
  252.4 13.2 %all-gather.2 = bf16[32,1,2]{2,1,0:T(2,128)(2,1)S(1)} all-gather(bf16[8,1,2]{2,1,0:T(2,128)(2,1)S(1)} %all-to-all-done.5), channel_id=4, replica_groups=mesh['pulse'=4,'tile'=8] {'pulse'}, dimensions={0}, use_global_device_ids=true | all-gather | bytes 160 | tf_op jit(solution)/shard_map/all_gather | solution.py:87
  265.7 4.2 all-to-all-start.1
  269.9 13.2 %all-gather.1 = bf16[32,1,2]{2,1,0:T(2,128)(2,1)S(1)} all-gather(bf16[8,1,2]{2,1,0:T(2,128)(2,1)S(1)} %all-to-all-done.3), channel_id=3, replica_groups=mesh['pulse'=4,'tile'=8] {'pulse'}, dimensions={0}, use_global_device_ids=true | all-gather | bytes 160 | tf_op jit(solution)/shard_map/all_gather | solution.py:87
  283.2 4.2 all-to-all-start.6
  287.4 13.2 %all-gather = bf16[32,1,2]{2,1,0:T(2,128)(2,1)S(1)} all-gather(bf16[8,1,2]{2,1,0:T(2,128)(2,1)S(1)} %all-to-all-done.1), channel_id=2, replica_groups=mesh['pulse'=4,'tile'=8] {'pulse'}, dimensions={0}, use_global_device_ids=true | all-gather | bytes 160 | tf_op jit(solution)/shard_map/all_gather | solution.py:87
  301.1 4.2 all-to-all-start.4
  305.3 13.4 %all_gather.42 = bf16[32,2,1024]{2,1,0:T(2,128)(2,1)S(1)} all-gather(bf16[8,2,1024]{2,1,0:T(2,128)(2,1)S(1)} %all-to-all-done.6), channel_id=1, replica_groups=mesh['pulse'=4,'tile'=8] {'pulse'}, dimensions={0}, use_global_device_ids=true | all-gather | bytes 163840 | tf_op jit(solution)/shard_map/all_gather | solution.py:86
  320.1 4.2 all-to-all-start.2
  324.3 13.4 %all_gather.40 = bf16[32,2,1024]{2,1,0:T(2,128)(2,1)S(1)} all-gather(bf16[8,2,1024]{2,1,0:T(2,128)(2,1)S(1)} %all-to-all-done.4), channel_id=1, replica_groups=mesh['pulse'=4,'tile'=8] {'pulse'}, dimensions={0}, use_global_device_ids=true | all-gather | bytes 163840 | tf_op jit(solution)/shard_map/all_gather | solution.py:86
  339.8 4.2 all-to-all-start
  344.0 13.4 %all_gather.38 = bf16[32,2,1024]{2,1,0:T(2,128)(2,1)S(1)} all-gather(bf16[8,2,1024]{2,1,0:T(2,128)(2,1)S(1)} %all-to-all-done.2), channel_id=1, replica_groups=mesh['pulse'=4,'tile'=8] {'pulse'}, dimensions={0}, use_global_device_ids=true | all-gather | bytes 163840 | tf_op jit(solution)/shard_map/all_gather | solution.py:86
  358.5 13.6 %all_gather.35 = bf16[32,2,1024]{2,1,0:T(2,128)(2,1)S(1)} all-gather(bf16[8,2,1024]{2,1,0:T(2,128)(2,1)S(1)} %all-to-all-done), channel_id=1, replica_groups=mesh['pulse'=4,'tile'=8] {'pulse'}, dimensions={0}, use_global_device_ids=true | all-gather | bytes 163840 | tf_op jit(solution)/shard_map/all_gather | solution.py:86
  376.4 3.6 copy.121
  380.0 3.9 broadcast_in_dim.159
  384.0 3.6 copy.115
  387.6 5.1 %add_reduce_fusion = f32[2,1024,4]{2,1,0:T(8,128)S(1)} fusion(f32[32,1024,4]{0,2,1:T(4,128)} %copy.123, f32[32,1024,4]{0,2,1:T(4,128)} %copy.122, f32[32,2,1024]{0,2,1:T(8,128)S(1)} %copy.120, f32[32,2,1024]{0,2,1:T(8,128)} %copy.114), kind=kLoop, calls=%fused_computation.52 | loop fusion | flops 1040384 | bytes 1605632 | tf_op jit(solution)/shard_map/reduce_sum | solution.py:91
  398.6 3.6 copy.111
  402.3 3.9 broadcast_in_dim.152
  406.2 3.6 copy.105
  409.8 5.1 %add_reduce_fusion.1 = f32[2,1024,4]{2,1,0:T(8,128)S(1)} fusion(f32[32,1024,4]{0,2,1:T(4,128)} %copy.113, f32[32,1024,4]{0,2,1:T(4,128)} %copy.112, f32[32,2,1024]{0,2,1:T(8,128)S(1)} %copy.110, f32[32,2,1024]{0,2,1:T(8,128)} %copy.104), kind=kLoop, calls=%fused_computation.53 | loop fusion | flops 1040384 | bytes 1605632 | tf_op jit(solution)/shard_map/reduce_sum | solution.py:91
  419.7 3.6 copy.101
  426.0 3.6 copy.95
  429.6 5.1 %add_reduce_fusion.2 = f32[2,1024,4]{2,1,0:T(8,128)S(1)} fusion(f32[32,1024,4]{0,2,1:T(4,128)} %copy.103, f32[32,1024,4]{0,2,1:T(4,128)} %copy.102, f32[32,2,1024]{0,2,1:T(8,128)S(1)} %copy.100, f32[32,2,1024]{0,2,1:T(8,128)S(1)} %copy.94), kind=kLoop, calls=%fused_computation.54 | loop fusion | flops 1040384 | bytes 1605632 | tf_op jit(solution)/shard_map/reduce_sum | solution.py:91
  435.9 5.0 %add_reduce_fusion.3 = f32[2,1024,4]{2,1,0:T(8,128)S(1)} fusion(f32[32,1024,4]{0,2,1:T(4,128)} %copy.93, f32[32,1024,4]{0,2,1:T(4,128)} %copy.92, f32[32,2,1024]{0,2,1:T(8,128)S(1)} %copy.90, f32[32,2,1024]{0,2,1:T(8,128)S(1)} %copy.84), kind=kLoop, calls=%fused_computation.55 | loop fusion | flops 1040384 | bytes 1605632 | tf_op jit(solution)/shard_map/reduce_sum | solution.py:91
  444.2 3.6 copy.91
  450.5 3.7 copy.85
  459.4 12.1 %all-reduce.7 = (f32[32]{0:T(128)S(1)}, f32[32]{0:T(128)S(1)}, f32[32]{0:T(128)S(1)}, f32[32]{0:T(128)S(1)}, f32[32]{0:T(128)S(1)}, /*index=5*/f32[32]{0:T(128)S(1)}, f32[32]{0:T(128)S(1)}, f32[32]{0:T(128)S(1)}) all-reduce(f32[32]{0:T(128)S(1)} %get-tuple-element.157, ...), channel_id=1, replica_groups=mesh['pulse'=4,'tile'=8] {'tile'}, use_global_device_ids=true, to_apply=%region_4.8 | all-reduce | flops 256 | bytes 2048 | tf_op jit(solution)/shard_map/psum | solution.py:93
  (318 shorter events, 134.0 us)
Async XLA Ops:
  13.9 6.3 %copy-start = (bf16[2,1024,2048]{2,1,0:T(8,128)(2,1)S(1)}, bf16[2,1024,2048]{2,1,0:T(8,128)(2,1)}, u32[]{:S(2)}) copy-start(bf16[2,1024,2048]{2,1,0:T(8,128)(2,1)} %param.14) | copy-start | bytes 25165828
  20.3 1.4 copy-start.25
  20.3 18.9 %copy-start.24 = (s32[1,4]{1,0:T(1,128)S(1)}, s32[1,4]{1,0:T(1,128)}, u32[]{:S(2)}) copy-start(s32[1,4]{1,0:T(1,128)} %param.18) | copy-start | bytes 52
  20.3 61.2 %copy-start.26 = (s32[4]{0:T(128)S(1)}, s32[4]{0:T(128)}, u32[]{:S(2)}) copy-start(s32[4]{0:T(128)} %param.17) | copy-start | bytes 52
  20.3 61.5 %copy-start.27 = (s32[4]{0:T(128)S(1)}, s32[4]{0:T(128)}, u32[]{:S(2)}) copy-start(s32[4]{0:T(128)} %param.16) | copy-start | bytes 52
  33.3 186.1 %all-to-all-start.7 = ((bf16[8,1,2]{2,1,0:T(2,128)(2,1)}), bf16[8,1,2]{2,1,0:T(2,128)(2,1)S(1)}, u32[]{:S(2)}, u32[]{:S(2)}) async-start(bf16[8,1,2]{2,1,0:T(2,128)(2,1)} %copy.117), calls=%async_computation.7 | async-start | bytes 8192 | tf_op jit(solution)/shard_map/all_to_all | solution.py:83
  219.4 28.9 %all-to-all-start.5 = ((bf16[8,1,2]{2,1,0:T(2,128)(2,1)}), bf16[8,1,2]{2,1,0:T(2,128)(2,1)S(1)}, u32[]{:S(2)}, u32[]{:S(2)}) async-start(bf16[8,1,2]{2,1,0:T(2,128)(2,1)} %copy.107), calls=%async_computation.5 | async-start | bytes 8192 | tf_op jit(solution)/shard_map/all_to_all | solution.py:83
  248.3 17.4 %all-to-all-start.3 = ((bf16[8,1,2]{2,1,0:T(2,128)(2,1)}), bf16[8,1,2]{2,1,0:T(2,128)(2,1)S(1)}, u32[]{:S(2)}, u32[]{:S(2)}) async-start(bf16[8,1,2]{2,1,0:T(2,128)(2,1)} %copy.97), calls=%async_computation.3 | async-start | bytes 8192 | tf_op jit(solution)/shard_map/all_to_all | solution.py:83
  265.7 17.5 %all-to-all-start.1 = ((bf16[8,1,2]{2,1,0:T(2,128)(2,1)}), bf16[8,1,2]{2,1,0:T(2,128)(2,1)S(1)}, u32[]{:S(2)}, u32[]{:S(2)}) async-start(bf16[8,1,2]{2,1,0:T(2,128)(2,1)} %copy.87), calls=%async_computation.1 | async-start | bytes 8192 | tf_op jit(solution)/shard_map/all_to_all | solution.py:83
  283.2 17.9 %all-to-all-start.6 = ((bf16[8,2,1024]{2,1,0:T(2,128)(2,1)}), bf16[8,2,1024]{2,1,0:T(2,128)(2,1)S(1)}, u32[]{:S(2)}, u32[]{:S(2)}) async-start(bf16[8,2,1024]{2,1,0:T(2,128)(2,1)} %slice_bitcast_fusion.8), calls=%async_computation.6 | async-start | bytes 65536 | tf_op jit(solution)/shard_map/all_to_all | solution.py:82
  301.1 19.0 %all-to-all-start.4 = ((bf16[8,2,1024]{2,1,0:T(2,128)(2,1)}), bf16[8,2,1024]{2,1,0:T(2,128)(2,1)S(1)}, u32[]{:S(2)}, u32[]{:S(2)}) async-start(bf16[8,2,1024]{2,1,0:T(2,128)(2,1)} %slice_bitcast_fusion.9), calls=%async_computation.4 | async-start | bytes 65536 | tf_op jit(solution)/shard_map/all_to_all | solution.py:82
  320.1 19.7 %all-to-all-start.2 = ((bf16[8,2,1024]{2,1,0:T(2,128)(2,1)}), bf16[8,2,1024]{2,1,0:T(2,128)(2,1)S(1)}, u32[]{:S(2)}, u32[]{:S(2)}) async-start(bf16[8,2,1024]{2,1,0:T(2,128)(2,1)} %slice_bitcast_fusion.10), calls=%async_computation.2 | async-start | bytes 65536 | tf_op jit(solution)/shard_map/all_to_all | solution.py:82
  339.8 18.6 %all-to-all-start = ((bf16[8,2,1024]{2,1,0:T(2,128)(2,1)}), bf16[8,2,1024]{2,1,0:T(2,128)(2,1)S(1)}, u32[]{:S(2)}, u32[]{:S(2)}) async-start(bf16[8,2,1024]{2,1,0:T(2,128)(2,1)} %slice_bitcast_fusion.11), calls=%async_computation | async-start | bytes 65536 | tf_op jit(solution)/shard_map/all_to_all | solution.py:82
  429.6 5.8 %copy-start.16 = (f32[32,2,1023]{2,1,0:T(2,128)S(1)}, f32[32,2,1023]{2,1,0:T(2,128)}, u32[]{:S(2)}) copy-start(f32[32,2,1023]{2,1,0:T(2,128)} %slice.397) | copy-start | bytes 785668
  447.7 6.4 %copy-start.2 = (f32[32,2,4096]{2,0,1:T(8,128)S(1)}, f32[32,2,4096]{2,0,1:T(8,128)}, u32[]{:S(2)}) copy-start(f32[32,2,4096]{2,0,1:T(8,128)} %copy.121) | copy-start | bytes 3145732
  447.8 6.4 %copy-start.3 = (f32[32,2,4096]{2,0,1:T(8,128)S(1)}, f32[32,2,4096]{2,0,1:T(8,128)}, u32[]{:S(2)}) copy-start(f32[32,2,4096]{2,0,1:T(8,128)} %copy.115) | copy-start | bytes 3145732
  450.4 5.3 %copy-start.22 = (f32[4096]{0:T(1024)S(1)}, f32[4096]{0:T(1024)}, u32[]{:S(2)}) copy-start(f32[4096]{0:T(1024)} %mul.561) | copy-start | bytes 49156
  450.5 5.3 %copy-start.23 = (f32[4096]{0:T(1024)S(1)}, f32[4096]{0:T(1024)}, u32[]{:S(2)}) copy-start(f32[4096]{0:T(1024)} %mul.564) | copy-start | bytes 49156
  450.5 5.6 %copy-start.4 = (f32[32,2,4096]{2,0,1:T(8,128)S(1)}, f32[32,2,4096]{2,0,1:T(8,128)}, u32[]{:S(2)}) copy-start(f32[32,2,4096]{2,0,1:T(8,128)} %copy.111) | copy-start | bytes 3145732
  454.2 1.9 copy-start.5
  454.2 1.9 copy-start.14
  454.2 1.9 copy-start.15
  455.7 2.4 copy-start.1
  455.7 1.7 copy-start.6
  455.7 2.0 copy-start.7
  455.8 2.1 copy-start.12
  455.8 2.2 copy-start.13
  456.3 2.1 copy-start.8
  456.3 2.3 copy-start.9
  456.3 2.4 copy-start.10
  456.4 2.6 copy-start.11
  459.1 14.4 %copy-start.20 = (bf16[1,64,128]{2,1,0:T(8,128)(2,1)S(1)}, bf16[1,64,128]{2,1,0:T(8,128)(2,1)}, u32[]{:S(2)}) copy-start(bf16[1,64,128]{2,1,0:T(8,128)(2,1)} %get-tuple-element.254) | copy-start | bytes 49156
  459.1 14.4 %copy-start.21 = (bf16[1,64,128]{2,1,0:T(8,128)(2,1)S(1)}, bf16[1,64,128]{2,1,0:T(8,128)(2,1)}, u32[]{:S(2)}) copy-start(bf16[1,64,128]{2,1,0:T(8,128)(2,1)} %get-tuple-element.255) | copy-start | bytes 49156
  473.1 1.2 copy-start.18
  473.1 1.2 copy-start.19
  475.0 0.7 copy-start.17
where the time goes:
time: 484 us; the launch traced here: 478 us
  blocking collectives  199 us (41%)
  local copies, waits for them, and re-layouts  142 us (29%)
  matrix products  46 us (10%)
  starting transfers between devices  45.2 us (9%)
  other arithmetic  35.4 us (7%)
  between operations  11 us (2%)
    all_gather x4, blocking collectives, shards(): lax.all_gather(mine_pieces, 'pulse', axis=0, tiled=True)  53.7 us
    all_gather x4, blocking collectives, shards(): lax.all_gather(mine_edges, 'pulse', axis=0, tiled=True)  53.4 us
    gather x96, local copies, waits for them, and re-layouts  44.3 us
    all_gather x1, blocking collectives, shards(): lax.all_gather(pulse_order, ('pulse', 'tile'), axis=0, tiled=True)  42.3 us
    unnamed x1, blocking collectives  37.2 us
    all_to_all x4, starting transfers between devices, shards(): lax.all_to_all(edges, 'tile', split_axis=0, concat_axis=0, tiled=True)  28.5 us
    reduce_sum x4, other arithmetic, shards(): summed = jnp.sum(samples, axis=0)  20.3 us
    all_to_all x4, starting transfers between devices, shards(): lax.all_to_all(pieces, 'tile', split_axis=0, concat_axis=0, tiled=True)  16.7 us
  transfers between devices with their start and end apart: 8, of which 0 were waited for; matrix products, arithmetic and copies ran while one was open for 22% of the time, Pallas kernels for 0%

commit v1 on v0

--- a/solution.py
+++ b/solution.py
@@ -7,6 +7,18 @@
 STEPS = 4
 PS = 1
 R_DEV = 128
+
+
+def collect(shard, axis, dim):
+    ways, here = (lax.axis_size(axis), lax.axis_index(axis))
+    grown, reach = (shard, 1)
+    while reach < ways:
+        theirs = lax.ppermute(grown, axis, [(d, d ^ reach) for d in range(ways)])
+        mine_first = jnp.concatenate([grown, theirs], axis=dim)
+        theirs_first = jnp.concatenate([theirs, grown], axis=dim)
+        grown = jnp.where(here & reach == 0, mine_first, theirs_first)
+        reach = 2 * reach
+    return grown
 
 
 def compress(windows, filt):
@@ -83,7 +95,7 @@
             lax.all_to_all(edges, "tile", split_axis=0, concat_axis=0, tiled=True),
         )
         pieces, edges = (
-            lax.all_gather(mine_pieces, "pulse", axis=0, tiled=True),
+            collect(mine_pieces, "pulse", 0),
             lax.all_gather(mine_edges, "pulse", axis=0, tiled=True),
         )
         shifts = jnp.take(all_fine, chosen)

time: 484 us -> 449 us (0.928)
  blocking collectives: 199 us -> 161 us
  starting transfers between devices: 45.2 us -> 34.8 us
  waiting for transfers between devices: 0.02 us -> 5.92 us
    all_gather x4 -> x0, blocking collectives: 53.7 us -> none  [shards(): lax.all_gather(mine_pieces, 'pulse', axis=0, tiled=True)]
    all_to_all x4 -> x2, starting transfers between devices: 28.5 us -> 8.75 us  [shards(): lax.all_to_all(edges, 'tile', split_axis=0, concat_axis=0, tiled=True)]
    all_to_all x0 -> x2, blocking collectives: none -> 15.7 us  [shards(): lax.all_to_all(edges, 'tile', split_axis=0, concat_axis=0, tiled=True)]
    ppermute x0 -> x8, starting transfers between devices: none -> 10.2 us  [collect(): theirs = lax.ppermute(grown, axis, [(d, d ^ reach) for d in range(ways)])]
  transfers between devices with their start and end apart: 8 -> 14, of which waited for: 0 -> 2; matrix products, arithmetic and copies ran while one was open for 22% -> 24% of each run, Pallas kernels for 0% -> 0%
where the time goes in v1:
time: 449 us; the launch traced here: 443 us
  blocking collectives  161 us (36%)
  local copies, waits for them, and re-layouts  146 us (33%)
  matrix products  46 us (10%)
  other arithmetic  38.6 us (9%)
  starting transfers between devices  34.8 us (8%)
  between operations  11.1 us (2%)
  waiting for transfers between devices  5.92 us (1%)
    all_gather x4, blocking collectives, shards(): lax.all_gather(mine_edges, 'pulse', axis=0, tiled=True)  53.4 us
    gather x96, local copies, waits for them, and re-layouts  44 us
    all_gather x1, blocking collectives, shards(): lax.all_gather(pulse_order, ('pulse', 'tile'), axis=0, tiled=True)  42.3 us
    unnamed x1, blocking collectives  37.3 us
    reduce_sum x4, other arithmetic, shards(): summed = jnp.sum(samples, axis=0)  20.3 us
    all_to_all x4, starting transfers between devices, shards(): lax.all_to_all(pieces, 'tile', split_axis=0, concat_axis=0, tiled=True)  15.8 us
    all_to_all x2, blocking collectives, shards(): lax.all_to_all(edges, 'tile', split_axis=0, concat_axis=0, tiled=True)  15.7 us
    reshape x4, local copies, waits for them, and re-layouts, interpolate(): first = jnp.repeat(first, 4, axis=-1)  14.7 us
  transfers between devices with their start and end apart: 14, of which 2 were waited for; matrix products, arithmetic and copies ran while one was open for 24% of the time, Pallas kernels for 0%

profile of v1, /device:TPU:0, one launch (start us, length us, event | category | flops | bytes accessed | tf_op | source)
XLA Modules:
  0.0 443.3 jit_solution(14845577191541846631)
XLA Ops:
  13.9 3.0 fusion.19
  16.9 3.3 fusion.3
  21.7 11.0 %while.17 = (s32[]{:T(128)}, bf16[1,2,2048]{2,1,0:T(2,128)(2,1)S(1)}, s32[8,3]{0,1:T(4,128)S(1)}, bf16[8,2,1025]{2,1,0:T(2,128)(2,1)S(1)}, s32[]{:T(128)}) while((s32[]{:T(128)}, bf16[1,2,2048]{2,1,0:T(2,128)(2,1)S(1)}, s32[8,3]{0,1:T(4,128)S(1)}, bf16[8,2,1025]{2,1,0:T(2,128)(2,1)S(1)}, s32[]{:T(128)}) %tuple.191), condition=%wide.while_cond.13, body=%wide.while_body.13.sunk | while | flops 2 | bytes 9321 | solution.py:37
  33.5 5.2 %all-to-all-start.7 = ((bf16[8,1,2]{2,1,0:T(2,128)(2,1)}), bf16[8,1,2]{2,1,0:T(2,128)(2,1)S(1)}, u32[]{:S(2)}, u32[]{:S(2)}) async-start(bf16[8,1,2]{2,1,0:T(2,128)(2,1)} %copy.117), calls=%async_computation.7 | async-start | bytes 8192 | tf_op jit(solution)/shard_map/all_to_all | solution.py:95
  39.3 42.3 %all-gather.4 = s32[32,1,4]{2,1,0:T(1,128)S(1)} all-gather(s32[1,1,4]{2,1,0:T(1,128)S(1)} %bitcast.332), channel_id=1, replica_groups=mesh['pulse'=4,'tile'=8] {'pulse','tile'}, dimensions={0}, use_global_device_ids=true | all-gather | bytes 528 | tf_op jit(solution)/shard_map/all_gather | solution.py:71
  82.2 37.3 %all-reduce.6 = (s32[128]{0:T(128)S(1)}, s32[128]{0:T(128)S(1)}) all-reduce(s32[128]{0:T(128)S(1)} %dynamic-update-slice.19, s32[128]{0:T(128)S(1)} %dynamic-update-slice.18), channel_id=1, replica_groups=mesh['pulse'=4,'tile'=8] {'pulse','tile'}, use_global_device_ids=true, to_apply=%add.5 | all-reduce | flops 256 | bytes 2048
  125.2 2.8 fusion.23
  128.0 2.8 fusion.7
  130.9 2.8 fusion.5
  133.7 2.8 fusion.21
  136.7 11.0 %while.16 = (s32[]{:T(128)}, bf16[1,2,2048]{2,1,0:T(2,128)(2,1)S(1)}, s32[8,3]{0,1:T(4,128)S(1)}, bf16[8,2,1025]{2,1,0:T(2,128)(2,1)S(1)}, s32[]{:T(128)}) while((s32[]{:T(128)}, bf16[1,2,2048]{2,1,0:T(2,128)(2,1)S(1)}, s32[8,3]{0,1:T(4,128)S(1)}, bf16[8,2,1025]{2,1,0:T(2,128)(2,1)S(1)}, s32[]{:T(128)}) %tuple.188), condition=%wide.while_cond.10, body=%wide.while_body.10.sunk | while | flops 2 | bytes 9321 | solution.py:37
  148.3 2.8 fusion.27
  151.2 2.8 fusion.11
  154.0 2.8 fusion.9
  156.8 2.8 fusion.25
  159.8 11.5 %while.15 = (s32[]{:T(128)}, bf16[1,2,2048]{2,1,0:T(2,128)(2,1)S(1)}, s32[8,3]{0,1:T(4,128)S(1)}, bf16[8,2,1025]{2,1,0:T(2,128)(2,1)S(1)}, s32[]{:T(128)}) while((s32[]{:T(128)}, bf16[1,2,2048]{2,1,0:T(2,128)(2,1)S(1)}, s32[8,3]{0,1:T(4,128)S(1)}, bf16[8,2,1025]{2,1,0:T(2,128)(2,1)S(1)}, s32[]{:T(128)}) %tuple.185), condition=%wide.while_cond.7, body=%wide.while_body.7.sunk | while | flops 2 | bytes 9321 | solution.py:37
  174.8 2.8 fusion.15
  177.7 2.8 fusion.13
  180.5 2.8 fusion.29
  183.5 10.6 %while.14 = (s32[]{:T(128)}, bf16[1,2,2048]{2,1,0:T(2,128)(2,1)S(1)}, s32[8,3]{0,1:T(4,128)S(1)}, bf16[8,2,1025]{2,1,0:T(2,128)(2,1)S(1)}, s32[]{:T(128)}) while((s32[]{:T(128)}, bf16[1,2,2048]{2,1,0:T(2,128)(2,1)S(1)}, s32[8,3]{0,1:T(4,128)S(1)}, bf16[8,2,1025]{2,1,0:T(2,128)(2,1)S(1)}, s32[]{:T(128)}) %tuple.182), condition=%wide.while_cond.4, body=%wide.while_body.4.sunk | while | flops 2 | bytes 9321 | solution.py:37
  218.5 3.6 all-to-all-start.5
  222.1 13.8 %all-gather.3 = bf16[32,1,2]{2,1,0:T(2,128)(2,1)S(1)} all-gather(bf16[8,1,2]{2,1,0:T(2,128)(2,1)S(1)} %all-to-all-done.7), channel_id=5, replica_groups=mesh['pulse'=4,'tile'=8] {'pulse'}, dimensions={0}, use_global_device_ids=true | all-gather | bytes 160 | tf_op jit(solution)/shard_map/all_gather | solution.py:99
  235.9 8.7 %all_to_all.68 = bf16[8,1,2]{2,1,0:T(2,128)(2,1)S(1)} all-to-all(bf16[8,1,2]{2,1,0:T(2,128)(2,1)S(1)} %copy.97), channel_id=1, replica_groups=mesh['pulse'=4,'tile'=8] {'tile'}, dimensions={0} | all-to-all | bytes 64 | tf_op jit(solution)/shard_map/all_to_all | solution.py:95
  244.6 7.0 %all_to_all.69 = bf16[8,1,2]{2,1,0:T(2,128)(2,1)S(1)} all-to-all(bf16[8,1,2]{2,1,0:T(2,128)(2,1)S(1)} %copy.87), channel_id=1, replica_groups=mesh['pulse'=4,'tile'=8] {'tile'}, dimensions={0} | all-to-all | bytes 64 | tf_op jit(solution)/shard_map/all_to_all | solution.py:95
  251.7 3.3 all-to-all-start.6
  255.0 13.2 %all-gather.2 = bf16[32,1,2]{2,1,0:T(2,128)(2,1)S(1)} all-gather(bf16[8,1,2]{2,1,0:T(2,128)(2,1)S(1)} %all-to-all-done.5), channel_id=4, replica_groups=mesh['pulse'=4,'tile'=8] {'pulse'}, dimensions={0}, use_global_device_ids=true | all-gather | bytes 160 | tf_op jit(solution)/shard_map/all_gather | solution.py:99
  268.3 4.1 all-to-all-start.4
  272.4 13.2 %all-gather.1 = bf16[32,1,2]{2,1,0:T(2,128)(2,1)S(1)} all-gather(bf16[8,1,2]{2,1,0:T(2,128)(2,1)S(1)} %all_to_all.68), channel_id=3, replica_groups=mesh['pulse'=4,'tile'=8] {'pulse'}, dimensions={0}, use_global_device_ids=true | all-gather | bytes 160 | tf_op jit(solution)/shard_map/all_gather | solution.py:99
  285.7 4.2 all-to-all-start.2
  289.9 13.2 %all-gather = bf16[32,1,2]{2,1,0:T(2,128)(2,1)S(1)} all-gather(bf16[8,1,2]{2,1,0:T(2,128)(2,1)S(1)} %all_to_all.69), channel_id=2, replica_groups=mesh['pulse'=4,'tile'=8] {'pulse'}, dimensions={0}, use_global_device_ids=true | all-gather | bytes 160 | tf_op jit(solution)/shard_map/all_gather | solution.py:99
  303.7 4.2 all-to-all-start
  321.0 3.5 collective-permute-done.7
  334.7 3.9 broadcast_in_dim.162
  338.6 3.6 copy.121
  342.2 3.9 broadcast_in_dim.159
  346.1 3.6 copy.115
  349.7 5.3 %add_reduce_fusion = f32[2,1024,4]{2,1,0:T(8,128)S(1)} fusion(f32[32,1024,4]{0,2,1:T(4,128)} %copy.123, f32[32,1024,4]{0,2,1:T(4,128)} %copy.122, f32[32,2,1024]{0,2,1:T(8,128)} %copy.120, f32[32,2,1024]{0,2,1:T(8,128)} %copy.114), kind=kLoop, calls=%fused_computation.52 | loop fusion | flops 1040384 | bytes 1605632 | tf_op jit(solution)/shard_map/reduce_sum | solution.py:103
  361.1 3.9 broadcast_in_dim.155
  365.0 3.6 copy.111
  371.3 3.8 copy.105
  375.1 5.1 %add_reduce_fusion.1 = f32[2,1024,4]{2,1,0:T(8,128)S(1)} fusion(f32[32,1024,4]{0,2,1:T(4,128)} %copy.113, f32[32,1024,4]{0,2,1:T(4,128)} %copy.112, f32[32,2,1024]{0,2,1:T(8,128)} %copy.110, f32[32,2,1024]{0,2,1:T(8,128)S(1)} %copy.104), kind=kLoop, calls=%fused_computation.53 | loop fusion | flops 1040384 | bytes 1605632 | tf_op jit(solution)/shard_map/reduce_sum | solution.py:103
  385.0 3.6 copy.101
  391.3 3.6 copy.95
  394.9 5.0 %add_reduce_fusion.2 = f32[2,1024,4]{2,1,0:T(8,128)S(1)} fusion(f32[32,1024,4]{0,2,1:T(4,128)} %copy.103, f32[32,1024,4]{0,2,1:T(4,128)} %copy.102, f32[32,2,1024]{0,2,1:T(8,128)S(1)} %copy.100, f32[32,2,1024]{0,2,1:T(8,128)S(1)} %copy.94), kind=kLoop, calls=%fused_computation.54 | loop fusion | flops 1040384 | bytes 1605632 | tf_op jit(solution)/shard_map/reduce_sum | solution.py:103
  401.0 5.0 %add_reduce_fusion.3 = f32[2,1024,4]{2,1,0:T(8,128)S(1)} fusion(f32[32,1024,4]{0,2,1:T(4,128)} %copy.93, f32[32,1024,4]{0,2,1:T(4,128)} %copy.92, f32[32,2,1024]{0,2,1:T(8,128)S(1)} %copy.90, f32[32,2,1024]{0,2,1:T(8,128)S(1)} %copy.84), kind=kLoop, calls=%fused_computation.55 | loop fusion | flops 1040384 | bytes 1605632 | tf_op jit(solution)/shard_map/reduce_sum | solution.py:103
  409.3 3.8 copy.91
  415.9 3.7 copy.85
  424.8 11.8 %all-reduce.7 = (f32[32]{0:T(128)S(1)}, f32[32]{0:T(128)S(1)}, f32[32]{0:T(128)S(1)}, f32[32]{0:T(128)S(1)}, f32[32]{0:T(128)S(1)}, /*index=5*/f32[32]{0:T(128)S(1)}, f32[32]{0:T(128)S(1)}, f32[32]{0:T(128)S(1)}) all-reduce(f32[32]{0:T(128)S(1)} %get-tuple-element.157, ...), channel_id=1, replica_groups=mesh['pulse'=4,'tile'=8] {'tile'}, use_global_device_ids=true, to_apply=%region_4.8 | all-reduce | flops 256 | bytes 2048 | tf_op jit(solution)/shard_map/psum | solution.py:105
  (336 shorter events, 144.4 us)
Async XLA Ops:
  13.9 6.3 %copy-start = (bf16[2,1024,2048]{2,1,0:T(8,128)(2,1)S(1)}, bf16[2,1024,2048]{2,1,0:T(8,128)(2,1)}, u32[]{:S(2)}) copy-start(bf16[2,1024,2048]{2,1,0:T(8,128)(2,1)} %param.14) | copy-start | bytes 25165828
  20.2 1.4 copy-start.25
  20.2 19.1 %copy-start.24 = (s32[1,4]{1,0:T(1,128)S(1)}, s32[1,4]{1,0:T(1,128)}, u32[]{:S(2)}) copy-start(s32[1,4]{1,0:T(1,128)} %param.18) | copy-start | bytes 52
  20.2 61.5 %copy-start.26 = (s32[4]{0:T(128)S(1)}, s32[4]{0:T(128)}, u32[]{:S(2)}) copy-start(s32[4]{0:T(128)} %param.17) | copy-start | bytes 52
  20.2 61.7 %copy-start.27 = (s32[4]{0:T(128)S(1)}, s32[4]{0:T(128)}, u32[]{:S(2)}) copy-start(s32[4]{0:T(128)} %param.16) | copy-start | bytes 52
  33.5 185.0 %all-to-all-start.7 = ((bf16[8,1,2]{2,1,0:T(2,128)(2,1)}), bf16[8,1,2]{2,1,0:T(2,128)(2,1)S(1)}, u32[]{:S(2)}, u32[]{:S(2)}) async-start(bf16[8,1,2]{2,1,0:T(2,128)(2,1)} %copy.117), calls=%async_computation.7 | async-start | bytes 8192 | tf_op jit(solution)/shard_map/all_to_all | solution.py:95
  218.5 17.4 %all-to-all-start.5 = ((bf16[8,1,2]{2,1,0:T(2,128)(2,1)}), bf16[8,1,2]{2,1,0:T(2,128)(2,1)S(1)}, u32[]{:S(2)}, u32[]{:S(2)}) async-start(bf16[8,1,2]{2,1,0:T(2,128)(2,1)} %copy.107), calls=%async_computation.5 | async-start | bytes 8192 | tf_op jit(solution)/shard_map/all_to_all | solution.py:95
  251.7 16.7 %all-to-all-start.6 = ((bf16[8,2,1024]{2,1,0:T(2,128)(2,1)}), bf16[8,2,1024]{2,1,0:T(2,128)(2,1)S(1)}, u32[]{:S(2)}, u32[]{:S(2)}) async-start(bf16[8,2,1024]{2,1,0:T(2,128)(2,1)} %slice_bitcast_fusion.8), calls=%async_computation.6 | async-start | bytes 65536 | tf_op jit(solution)/shard_map/all_to_all | solution.py:94
  268.3 17.4 %all-to-all-start.4 = ((bf16[8,2,1024]{2,1,0:T(2,128)(2,1)}), bf16[8,2,1024]{2,1,0:T(2,128)(2,1)S(1)}, u32[]{:S(2)}, u32[]{:S(2)}) async-start(bf16[8,2,1024]{2,1,0:T(2,128)(2,1)} %slice_bitcast_fusion.9), calls=%async_computation.4 | async-start | bytes 65536 | tf_op jit(solution)/shard_map/all_to_all | solution.py:94
  285.7 18.0 %all-to-all-start.2 = ((bf16[8,2,1024]{2,1,0:T(2,128)(2,1)}), bf16[8,2,1024]{2,1,0:T(2,128)(2,1)S(1)}, u32[]{:S(2)}, u32[]{:S(2)}) async-start(bf16[8,2,1024]{2,1,0:T(2,128)(2,1)} %slice_bitcast_fusion.10), calls=%async_computation.2 | async-start | bytes 65536 | tf_op jit(solution)/shard_map/all_to_all | solution.py:94
  303.2 11.1 %collective-permute-start.6 = (bf16[8,2,1024]{2,1,0:T(2,128)(2,1)S(1)}, bf16[8,2,1024]{2,1,0:T(2,128)(2,1)S(1)}, u32[]{:S(2)}, u32[]{:S(2)}) collective-permute-start(bf16[8,2,1024]{2,1,0:T(2,128)(2,1)S(1)} %all-to-all-done.6), channel_id=1, source_target_pairs={{0,8},{8,0},{16,24},{24,16},{1,9},{9,1},{17,25},{25,17},{2,10},{10... | collective-permute-start | bytes 98312 | tf_op jit(solution)/shard_map/ppermute | solution.py:16
  303.7 9.0 %all-to-all-start = ((bf16[8,2,1024]{2,1,0:T(2,128)(2,1)}), bf16[8,2,1024]{2,1,0:T(2,128)(2,1)S(1)}, u32[]{:S(2)}, u32[]{:S(2)}) async-start(bf16[8,2,1024]{2,1,0:T(2,128)(2,1)} %slice_bitcast_fusion.11), calls=%async_computation | async-start | bytes 65536 | tf_op jit(solution)/shard_map/all_to_all | solution.py:94
  308.3 7.0 %collective-permute-start.4 = (bf16[8,2,1024]{2,1,0:T(2,128)(2,1)S(1)}, bf16[8,2,1024]{2,1,0:T(2,128)(2,1)S(1)}, u32[]{:S(2)}, u32[]{:S(2)}) collective-permute-start(bf16[8,2,1024]{2,1,0:T(2,128)(2,1)S(1)} %all-to-all-done.4), channel_id=1, source_target_pairs={{0,8},{8,0},{16,24},{24,16},{1,9},{9,1},{17,25},{25,17},{2,10},{10... | collective-permute-start | bytes 98312 | tf_op jit(solution)/shard_map/ppermute | solution.py:16
  309.9 7.7 %collective-permute-start.2 = (bf16[8,2,1024]{2,1,0:T(2,128)(2,1)S(1)}, bf16[8,2,1024]{2,1,0:T(2,128)(2,1)S(1)}, u32[]{:S(2)}, u32[]{:S(2)}) collective-permute-start(bf16[8,2,1024]{2,1,0:T(2,128)(2,1)S(1)} %all-to-all-done.2), channel_id=1, source_target_pairs={{0,8},{8,0},{16,24},{24,16},{1,9},{9,1},{17,25},{25,17},{2,10},{10... | collective-permute-start | bytes 98312 | tf_op jit(solution)/shard_map/ppermute | solution.py:16
  312.8 6.0 %collective-permute-start = (bf16[8,2,1024]{2,1,0:T(2,128)(2,1)S(1)}, bf16[8,2,1024]{2,1,0:T(2,128)(2,1)S(1)}, u32[]{:S(2)}, u32[]{:S(2)}) collective-permute-start(bf16[8,2,1024]{2,1,0:T(2,128)(2,1)S(1)} %all-to-all-done), channel_id=1, source_target_pairs={{0,8},{8,0},{16,24},{24,16},{1,9},{9,1},{17,25},{25,17},{2,10},{10... | collective-permute-start | bytes 98312 | tf_op jit(solution)/shard_map/ppermute | solution.py:16
  314.5 10.1 %collective-permute-start.7 = (bf16[16,2,1024]{2,1,0:T(2,128)(2,1)S(1)}, bf16[16,2,1024]{2,1,0:T(2,128)(2,1)S(1)}, u32[]{:S(2)}, u32[]{:S(2)}) collective-permute-start(bf16[16,2,1024]{2,1,0:T(2,128)(2,1)S(1)} %broadcast_select_fusion.4), channel_id=1, source_target_pairs={{0,16},{8,24},{16,0},{24,8},{1,17},{9,25},{17,1},{25,9},{2,18},{10... | collective-permute-start | bytes 196616 | tf_op jit(solution)/shard_map/ppermute | solution.py:16
  315.5 11.7 %collective-permute-start.5 = (bf16[16,2,1024]{2,1,0:T(2,128)(2,1)S(1)}, bf16[16,2,1024]{2,1,0:T(2,128)(2,1)S(1)}, u32[]{:S(2)}, u32[]{:S(2)}) collective-permute-start(bf16[16,2,1024]{2,1,0:T(2,128)(2,1)S(1)} %broadcast_select_fusion.5), channel_id=1, source_target_pairs={{0,16},{8,24},{16,0},{24,8},{1,17},{9,25},{17,1},{25,9},{2,18},{10... | collective-permute-start | bytes 196616 | tf_op jit(solution)/shard_map/ppermute | solution.py:16
  317.8 11.1 %collective-permute-start.3 = (bf16[16,2,1024]{2,1,0:T(2,128)(2,1)S(1)}, bf16[16,2,1024]{2,1,0:T(2,128)(2,1)S(1)}, u32[]{:S(2)}, u32[]{:S(2)}) collective-permute-start(bf16[16,2,1024]{2,1,0:T(2,128)(2,1)S(1)} %broadcast_select_fusion.6), channel_id=1, source_target_pairs={{0,16},{8,24},{16,0},{24,8},{1,17},{9,25},{17,1},{25,9},{2,18},{10... | collective-permute-start | bytes 196616 | tf_op jit(solution)/shard_map/ppermute | solution.py:16
  318.9 11.7 %collective-permute-start.1 = (bf16[16,2,1024]{2,1,0:T(2,128)(2,1)S(1)}, bf16[16,2,1024]{2,1,0:T(2,128)(2,1)S(1)}, u32[]{:S(2)}, u32[]{:S(2)}) collective-permute-start(bf16[16,2,1024]{2,1,0:T(2,128)(2,1)S(1)} %broadcast_select_fusion.7), channel_id=1, source_target_pairs={{0,16},{8,24},{16,0},{24,8},{1,17},{9,25},{17,1},{25,9},{2,18},{10... | collective-permute-start | bytes 196616 | tf_op jit(solution)/shard_map/ppermute | solution.py:16
  394.9 5.6 %copy-start.16 = (f32[32,2,1023]{2,1,0:T(2,128)S(1)}, f32[32,2,1023]{2,1,0:T(2,128)}, u32[]{:S(2)}) copy-start(f32[32,2,1023]{2,1,0:T(2,128)} %slice.397) | copy-start | bytes 785668
  413.2 6.4 %copy-start.2 = (f32[32,2,4096]{2,0,1:T(8,128)S(1)}, f32[32,2,4096]{2,0,1:T(8,128)}, u32[]{:S(2)}) copy-start(f32[32,2,4096]{2,0,1:T(8,128)} %copy.121) | copy-start | bytes 3145732
  413.2 6.4 %copy-start.3 = (f32[32,2,4096]{2,0,1:T(8,128)S(1)}, f32[32,2,4096]{2,0,1:T(8,128)}, u32[]{:S(2)}) copy-start(f32[32,2,4096]{2,0,1:T(8,128)} %copy.115) | copy-start | bytes 3145732
  415.9 5.6 %copy-start.4 = (f32[32,2,4096]{2,0,1:T(8,128)S(1)}, f32[32,2,4096]{2,0,1:T(8,128)}, u32[]{:S(2)}) copy-start(f32[32,2,4096]{2,0,1:T(8,128)} %copy.111) | copy-start | bytes 3145732
  419.6 1.9 copy-start.5
  419.6 1.9 copy-start.14
  419.6 1.9 copy-start.15
  421.1 2.4 copy-start.1
  421.1 1.7 copy-start.6
  421.1 2.0 copy-start.7
  421.1 2.1 copy-start.12
  421.1 2.2 copy-start.13
  421.7 2.1 copy-start.8
  421.7 2.3 copy-start.9
  421.7 2.4 copy-start.10
  421.7 2.6 copy-start.11
  424.5 14.2 %copy-start.22 = (bf16[1,64,128]{2,1,0:T(8,128)(2,1)S(1)}, bf16[1,64,128]{2,1,0:T(8,128)(2,1)}, u32[]{:S(2)}) copy-start(bf16[1,64,128]{2,1,0:T(8,128)(2,1)} %get-tuple-element.254) | copy-start | bytes 49156
  424.5 14.2 %copy-start.23 = (bf16[1,64,128]{2,1,0:T(8,128)(2,1)S(1)}, bf16[1,64,128]{2,1,0:T(8,128)(2,1)}, u32[]{:S(2)}) copy-start(bf16[1,64,128]{2,1,0:T(8,128)(2,1)} %get-tuple-element.255) | copy-start | bytes 49156
  438.2 1.2 copy-start.20
  438.2 1.2 copy-start.21
  439.4 0.7 copy-start.17
  440.2 0.8 copy-start.18
  440.2 0.8 copy-start.19
